TPU v7x, 256 devices: a whole 4x4x8 slice. The times are simulated.
256 devices in a mesh: xy: 32 (over z, x_lo, core), gz: 8 (over y, x_hi).
Axes of the slice: x: 4 (x_hi: 2, x_lo: 2; x = x_hi * 2 + x_lo), y: 4, z: 8, core: 2. Of those that a mesh axis runs over, the one named last changes fastest.
Arguments:
- file_data: float32 [512, 64, 8192], P('gz', None, 'xy')
- factor: float32 [512, 256], P('gz'), may hold values from -0.25 to 0.25
- block_owner: int32 [64], replicated, may hold values from 0 to 31, as said below
- block_offset: int32 [64], replicated, may hold values from 0 to 128, as said below
Outputs:
- gram: float32 [512, 512], P('gz')
- core: float32 [256, 64, 8192], P('gz', None, 'xy')
Inputs may be any that keep to these rules, and one draw needn't show every extreme that they name: `block_owner`: block b of device d (b = d * 2 + j) is owned by d - 1, d or d + 1 modulo 32. Every index of xy owns exactly 2 blocks. `block_offset`: offsets are multiples of 128; the blocks of one owner take distinct offsets, so every file slot is named once.
All inputs are finite; a program needn't handle non-finite values.
Results may differ from a plain program's by a relative error of at most 0.00007.
Values sent between devices are 32-bit elements; how exact they have to be, the bound alone decides.
A program may use at most 128 MiB of HBM per device.

v0:
```python
import jax
import jax.numpy as jnp
from jax import lax
from jax.sharding import PartitionSpec as P

BLOCKS_DEV = 2


def shifted(array, axis, by):
    length = lax.axis_size(axis)
    return lax.ppermute(array, axis, [(i, (i + by) % length) for i in range(length)])


def take_block(buffer, offset):
    return lax.dynamic_slice_in_dim(buffer, offset, 128, 2)


def rebalance(buffer, block_owner, block_offset):
    devices = lax.axis_size("xy")
    myself = lax.axis_index("xy")
    lower_peer = (myself + devices - 1) % devices
    upper_peer = (myself + 1) % devices

    def outgoing(target):
        pieces = []
        for j in range(BLOCKS_DEV):
            pieces.append(take_block(buffer, block_offset[target * BLOCKS_DEV + j]))
        return jnp.concatenate(pieces, axis=2)

    from_lower = shifted(outgoing(upper_peer), "xy", 1)
    from_upper = shifted(outgoing(lower_peer), "xy", -1)
    blocks = []
    for j in range(BLOCKS_DEV):
        owner = block_owner[myself * BLOCKS_DEV + j]
        offset = block_offset[myself * BLOCKS_DEV + j]
        local_block = take_block(buffer, offset)
        lower_block = from_lower[:, :, j * 128 : (j + 1) * 128]
        upper_block = from_upper[:, :, j * 128 : (j + 1) * 128]
        remote = jnp.where(owner == lower_peer, lower_block, upper_block)
        blocks.append(jnp.where(owner == myself, local_block, remote))
    return jnp.concatenate(blocks, axis=2)


def halves(x):
    high = lax.reduce_precision(x, exponent_bits=8, mantissa_bits=7)
    low = x - high
    return (high.astype(jnp.bfloat16), low.astype(jnp.bfloat16))


def dot(spec, a, b):
    return jnp.einsum(spec, a, b, preferred_element_type=jnp.float32)


def local(file_data, factor, block_owner, block_offset):
    whole_factor = lax.all_gather(factor, "gz", axis=0, tiled=True)
    swapped = lax.all_to_all(file_data, "gz", split_axis=1, concat_axis=0, tiled=True)
    scale = 1.0 / (BLOCKS_DEV * 128 * lax.axis_size("xy") * file_data.shape[1])
    high, low = halves(swapped)
    factor_high, factor_low = halves(whole_factor)
    core_part = (
        dot("zr,zcs->rcs", factor_high, high)
        + dot("zr,zcs->rcs", factor_high, low)
        + dot("zr,zcs->rcs", factor_low, high)
    )
    core = lax.all_to_all(core_part, "gz", split_axis=0, concat_axis=1, tiled=True)
    cross = dot("zcs,wcs->zw", high, low)
    partial_gram = (dot("zcs,wcs->zw", high, high) + (cross + cross.T)) * scale
    gram = lax.psum_scatter(partial_gram, "gz", scatter_dimension=0, tiled=True)
    gram = lax.psum(gram, "xy")
    core = rebalance(core, block_owner, block_offset)
    return (gram, core)


def solution(mesh):
    return jax.shard_map(
        local,
        mesh=mesh,
        in_specs=(P("gz", None, "xy"), P("gz", None), P(), P()),
        out_specs=(P("gz", None), P("gz", None, "xy")),
        check_vma=False,
    )
```

profile of v0, /device:TPU:4, one launch (start us, length us, event | category | flops | bytes accessed | tf_op | source)
XLA Modules:
  0.0 449.4 jit_solution(16877087336601075316)
XLA Ops:
  7.2 6.6 %copy.13 = f32[64,64,256]{2,0,1:T(8,128)} copy(f32[64,64,256]{2,1,0:T(8,128)} %param.4) | data formatting | bytes 8388608 | tf_op args[0]
  13.8 7.6 %all-to-all-start = ((f32[64,64,256]{2,0,1:T(8,128)}), f32[64,64,256]{2,0,1:T(8,128)}, u32[]{:S(2)}, u32[]{:S(2)}) async-start(f32[64,64,256]{2,0,1:T(8,128)} %copy.13), calls=%async_computation | async-start | bytes 8388608 | tf_op jit(solution)/shard_map/all_to_all | solution.py:56
  21.3 74.6 %all_gather.3 = f32[512,256]{1,0:T(8,128)S(1)} all-gather(f32[64,256]{1,0:T(8,128)S(1)} %copy-done.2), channel_id=1, replica_groups=mesh['xy'=32,'gz'=8] {'gz'}, dimensions={0}, use_global_device_ids=true | all-gather | bytes 589824 | tf_op jit(solution)/shard_map/all_gather | solution.py:55
  96.2 2.5 copy.14
  98.6 1.0 fusion.1
  100.4 0.7 fusion.13
  101.1 0.8 fusion.2
  101.9 2.6 copy.21
  104.5 8.9 %all-to-all-start.1 = ((f32[256,8,256]{2,1,0:T(8,128)}), f32[256,8,256]{2,1,0:T(8,128)S(1)}, u32[]{:S(2)}, u32[]{:S(2)}) async-start(f32[256,8,256]{2,1,0:T(8,128)} %copy.21), calls=%async_computation.2 | async-start | bytes 4194304 | tf_op jit(solution)/shard_map/all_to_all | solution.py:65
  121.5 3.1 fusion
  124.7 1.3 copy-done.1
  126.0 1.3 convolution_bitcast_fusion
  127.3 1.3 copy.15
  128.6 4.8 %fusion.4 = f32[512,512]{1,0:T(8,128)} fusion(bf16[512,8,256]{2,0,1:T(8,128)(2,1)} %bitcast.59, f32[512,512]{1,0:T(8,128)S(1)} %convolution_bitcast_fusion, f32[512,512]{0,1:T(8,128)} %copy.15), kind=kOutput, calls=%fused_computation.15 | convolution fusion | flops 1074528256 | bytes 5242880 | tf_op jit(solution)/shard_map/zcs,wcs->zw/dot_general | solution.py:51
  133.5 1.3 copy-done
  134.8 1.9 copy.30
  136.6 1.2 constant_dynamic-slice_fusion.3
  137.8 1.5 pad_maximum_fusion.1
  139.3 1.5 pad_maximum_fusion
  147.6 85.8 %reduce-scatter.2.cloned.1.call-done = f32[64,512]{1,0:T(8,128)} async-done(((f32[512,512]{1,0:T(8,128)}), f32[64,512]{1,0:T(8,128)}) %reduce-scatter.2.cloned.1.call-update) | async-done | bytes 131088 | tf_op jit(solution)/shard_map/reduce_scatter | solution.py:68
  233.5 2.9 fusion.6
  236.4 1.5 pad_maximum_fusion.2
  237.9 203.1 %all-reduce.2.cloned.1.call-done = f32[64,512]{1,0:T(8,128)} async-done(((f32[64,512]{1,0:T(8,128)}), f32[64,512]{1,0:T(8,128)}) %all-reduce.2.cloned.1.call-update) | async-done | bytes 131088 | tf_op jit(solution)/shard_map/psum | solution.py:69
  441.0 1.6 copy.32
  (21 shorter events, 2.2 us)
Async XLA Ops:
  13.8 7.6 %copy-start.2 = (f32[64,256]{1,0:T(8,128)S(1)}, f32[64,256]{1,0:T(8,128)}, u32[]{:S(2)}) copy-start(f32[64,256]{1,0:T(8,128)} %param.5) | copy-start | bytes 196612
  13.8 82.4 %all-to-all-start = ((f32[64,64,256]{2,0,1:T(8,128)}), f32[64,64,256]{2,0,1:T(8,128)}, u32[]{:S(2)}, u32[]{:S(2)}) async-start(f32[64,64,256]{2,0,1:T(8,128)} %copy.13), calls=%async_computation | async-start | bytes 8388608 | tf_op jit(solution)/shard_map/all_to_all | solution.py:56
  104.5 8.9 %copy-start.3 = (s32[64]{0:T(128)S(1)}, s32[64]{0:T(128)}, u32[]{:S(2)}) copy-start(s32[64]{0:T(128)} %param.7) | copy-start | bytes 772
  104.5 8.9 %copy-start.4 = (s32[64]{0:T(128)S(1)}, s32[64]{0:T(128)}, u32[]{:S(2)}) copy-start(s32[64]{0:T(128)} %param.6) | copy-start | bytes 772
  104.5 29.0 %all-to-all-start.1 = ((f32[256,8,256]{2,1,0:T(8,128)}), f32[256,8,256]{2,1,0:T(8,128)S(1)}, u32[]{:S(2)}, u32[]{:S(2)}) async-start(f32[256,8,256]{2,1,0:T(8,128)} %copy.21), calls=%async_computation.2 | async-start | bytes 4194304 | tf_op jit(solution)/shard_map/all_to_all | solution.py:65
  113.4 120.0 %reduce-scatter.2.cloned.1.call-start = ((), (), s32[]{:S(2)}) async-start(), calls=%async_computation.3 | async-start | bytes 1179648 | tf_op jit(solution)/shard_map/reduce_scatter | solution.py:68
  124.7 1.3 copy-start.1
  133.4 307.6 %all-reduce.2.cloned.1.call-start = ((), (), s32[]{:S(2)}) async-start(), calls=%async_computation.4 | async-start | bytes 262144 | tf_op jit(solution)/shard_map/psum | solution.py:69
  133.4 1.3 copy-start
  139.3 94.2 %collective-permute-start.1 = (f32[32,64,256]{2,1,0:T(8,128)}, f32[32,64,256]{2,1,0:T(8,128)}, u32[]{:S(2)}, u32[]{:S(2)}) collective-permute-start(f32[32,64,256]{2,1,0:T(8,128)} %pad_maximum_fusion.1), channel_id=1, source_target_pairs={{0,248},{8,0},{16,8},{24,16},{32,24},{40,32},{48,40},{56,48},{64,5... | collective-permute-start | bytes 6291464 | tf_op jit(solution)/shard_map/ppermute | solution.py:11
  140.8 92.6 %collective-permute-start = (f32[32,64,256]{2,1,0:T(8,128)}, f32[32,64,256]{2,1,0:T(8,128)}, u32[]{:S(2)}, u32[]{:S(2)}) collective-permute-start(f32[32,64,256]{2,1,0:T(8,128)} %pad_maximum_fusion), channel_id=1, source_target_pairs={{0,8},{8,16},{16,24},{24,32},{32,40},{40,48},{48,56},{56,64},{64,7... | collective-permute-start | bytes 6291464 | tf_op jit(solution)/shard_map/ppermute | solution.py:11
Sparse Core Ops, SparseCore 0:
  133.5 99.8 reduce-scatter.1
  236.0 204.9 all-reduce.1
where the time goes:
time: 450 us; the launch traced here: 449 us
  waiting for transfers between devices  289 us (64%)
  blocking collectives  74.6 us (17%)
  between operations  27.9 us (6%)
  local copies, waits for them, and re-layouts  21.1 us (5%)
  starting transfers between devices  17 us (4%)
  other arithmetic  11.6 us (3%)
  matrix products  8.25 us (2%)
    psum x1, waiting for transfers between devices, local(): gram = lax.psum(gram, 'xy')  203 us
    reduce_scatter x1, waiting for transfers between devices, local(): gram = lax.psum_scatter(partial_gram, 'gz', scatter_dimension=0, tiled=True)  85.8 us
    all_gather x1, blocking collectives, local(): whole_factor = lax.all_gather(factor, 'gz', axis=0, tiled=True)  74.6 us
    unnamed x12, local copies, waits for them, and re-layouts  10.8 us
  transfers between devices with their start and end apart: 6, of which 2 were waited for; matrix products, arithmetic and copies ran while one was open for 5% of the time, Pallas kernels for 0%

commit v1 on v0

--- a/solution.py
+++ b/solution.py
@@ -66,7 +66,7 @@
     cross = dot("zcs,wcs->zw", high, low)
     partial_gram = (dot("zcs,wcs->zw", high, high) + (cross + cross.T)) * scale
     gram = lax.psum_scatter(partial_gram, "gz", scatter_dimension=0, tiled=True)
-    gram = lax.psum(gram, "xy")
+    gram = jnp.sum(lax.all_gather(gram, "xy"), axis=0)
     core = rebalance(core, block_owner, block_offset)
     return (gram, core)
 

time: 450 us -> 303 us (0.67)
  the two profiles are of different devices: /device:TPU:4 before, /device:TPU:1 now
where the time goes in v1:
time: 303 us; the launch traced here: 302 us
  waiting for transfers between devices  138 us (46%)
  blocking collectives  88.5 us (29%)
  between operations  27.6 us (9%)
  local copies, waits for them, and re-layouts  17.4 us (6%)
  other arithmetic  12.4 us (4%)
  starting transfers between devices  11.1 us (4%)
  matrix products  6.99 us (2%)
    reduce_scatter x1, waiting for transfers between devices, local(): gram = lax.psum_scatter(partial_gram, 'gz', scatter_dimension=0, tiled=True)  75.8 us
    all_to_all x1, blocking collectives, local(): lax.all_to_all(file_data, 'gz', split_axis=1, concat_axis=0, tiled=True)  57.3 us
    ppermute x2, waiting for transfers between devices, shifted(): lax.ppermute(array, axis, [(i, (i + by) % length) for i in range(length)])  38.8 us
    all_gather x1, blocking collectives, local(): whole_factor = lax.all_gather(factor, 'gz', axis=0, tiled=True)  31.2 us
    all_to_all x1, waiting for transfers between devices, local(): lax.all_to_all(core_part, 'gz', split_axis=0, concat_axis=1, tiled=True)  23.4 us
    ppermute x2, starting transfers between devices, shifted(): lax.ppermute(array, axis, [(i, (i + by) % length) for i in range(length)])  7.28 us
    unnamed x11, local copies, waits for them, and re-layouts  7.12 us
    dot_general x5, matrix products, dot(): return jnp.einsum(spec, a, b, preferred_element_type=jnp.float32)  6.99 us
  transfers between devices with their start and end apart: 5, of which 3 were waited for; matrix products, arithmetic and copies ran while one was open for 6% of the time, Pallas kernels for 0%

profile of v1, /device:TPU:1, one launch (start us, length us, event | category | flops | bytes accessed | tf_op | source)
XLA Modules:
  0.0 302.1 jit_solution(1193531740150147953)
XLA Ops:
  7.2 4.6 %copy.13 = f32[64,64,256]{2,0,1:T(8,128)S(1)} copy(f32[64,64,256]{2,1,0:T(8,128)} %param.4) | data formatting | bytes 8388608 | tf_op args[0]
  11.8 57.3 %all_to_all.36 = f32[64,64,256]{2,0,1:T(8,128)S(1)} all-to-all(f32[64,64,256]{2,0,1:T(8,128)S(1)} %copy.13), channel_id=1, replica_groups=mesh['xy'=32,'gz'=8] {'gz'}, dimensions={1} | all-to-all | bytes 8388608 | tf_op jit(solution)/shard_map/all_to_all | solution.py:56
  70.0 1.2 copy-done
  71.1 1.3 convolution_bitcast_fusion
  72.4 1.3 copy.15
  73.7 3.5 %fusion.4 = f32[512,512]{1,0:T(8,128)} fusion(bf16[512,8,256]{2,0,1:T(8,128)(2,1)S(1)} %bitcast.63, f32[512,512]{1,0:T(8,128)S(1)} %convolution_bitcast_fusion, f32[512,512]{0,1:T(8,128)} %copy.15), kind=kOutput, calls=%fused_computation.15 | convolution fusion | flops 1074528256 | bytes 5242880 | tf_op jit(solution)/shard_map/zcs,wcs->zw/dot_general | solution.py:51
  77.3 75.8 %reduce-scatter.2.cloned.1.call-done = f32[64,512]{1,0:T(8,128)} async-done(((f32[512,512]{1,0:T(8,128)}), f32[64,512]{1,0:T(8,128)}) %reduce-scatter.2.cloned.1.call-update) | async-done | bytes 131088 | tf_op jit(solution)/shard_map/reduce_scatter | solution.py:68
  153.2 31.2 %all_gather.11 = f32[512,256]{1,0:T(8,128)S(1)} all-gather(f32[64,256]{1,0:T(8,128)S(1)} %copy-done.2), channel_id=1, replica_groups=mesh['xy'=32,'gz'=8] {'gz'}, dimensions={0}, use_global_device_ids=true | all-gather | bytes 589824 | tf_op jit(solution)/shard_map/all_gather | solution.py:55
  184.6 2.5 copy.14
  187.0 1.0 fusion.1
  190.3 2.5 copy.21
  192.9 3.7 %all-to-all-start.1 = ((f32[256,8,256]{2,1,0:T(8,128)}), f32[256,8,256]{2,1,0:T(8,128)S(1)}, u32[]{:S(2)}, u32[]{:S(2)}) async-start(f32[256,8,256]{2,1,0:T(8,128)} %copy.21), calls=%async_computation.2 | async-start | bytes 4194304 | tf_op jit(solution)/shard_map/all_to_all | solution.py:65
  204.7 23.4 %all-to-all-done.1 = f32[256,8,256]{2,1,0:T(8,128)S(1)} async-done(((f32[256,8,256]{2,1,0:T(8,128)}), f32[256,8,256]{2,1,0:T(8,128)S(1)}, u32[]{:S(2)}, u32[]{:S(2)}) %all-to-all-start.1) | async-done | bytes 2097184 | tf_op jit(solution)/shard_map/all_to_all | solution.py:65
  228.1 1.3 copy-done.1
  229.4 1.9 copy.30
  231.2 1.2 constant_dynamic-slice_fusion.3
  232.4 1.5 pad_maximum_fusion.1
  233.9 5.8 %collective-permute-start.1 = (f32[32,64,256]{2,1,0:T(8,128)}, f32[32,64,256]{2,1,0:T(8,128)}, u32[]{:S(2)}, u32[]{:S(2)}) collective-permute-start(f32[32,64,256]{2,1,0:T(8,128)} %pad_maximum_fusion.1), channel_id=1, source_target_pairs={{0,248},{8,0},{16,8},{24,16},{32,24},{40,32},{48,40},{56,48},{64,5... | collective-permute-start | bytes 6291464 | tf_op jit(solution)/shard_map/ppermute | solution.py:11
  239.7 1.5 pad_maximum_fusion
  241.2 1.5 collective-permute-start
  248.8 38.8 %collective-permute-done.1 = f32[32,64,256]{2,1,0:T(8,128)} collective-permute-done((f32[32,64,256]{2,1,0:T(8,128)}, f32[32,64,256]{2,1,0:T(8,128)}, u32[]{:S(2)}, u32[]{:S(2)}) %collective-permute-start.1) | collective-permute-done | bytes 2097184 | tf_op jit(solution)/shard_map/ppermute | solution.py:11
  287.7 2.9 fusion.6
  290.6 1.5 pad_maximum_fusion.2
  292.1 3.2 %reduce_sum.9 = f32[64,512]{1,0:T(8,128)} reduce(f32[32,64,512]{2,1,0:T(8,128)} %bitcast.61, f32[]{:T(128)} %constant.31.clone.1), dimensions={0}, to_apply=%region_1.0 | reduce | flops 1015808 | bytes 4325380 | tf_op jit(solution)/shard_map/reduce_sum | solution.py:69
  (20 shorter events, 4.0 us)
Async XLA Ops:
  7.2 146.0 %reduce-scatter.2.cloned.1.call-start = ((), (), s32[]{:S(2)}) async-start(), calls=%async_computation.3 | async-start | bytes 1179648 | tf_op jit(solution)/shard_map/reduce_scatter | solution.py:68
  69.2 2.0 copy-start
  73.7 79.5 %copy-start.2 = (f32[64,256]{1,0:T(8,128)S(1)}, f32[64,256]{1,0:T(8,128)}, u32[]{:S(2)}) copy-start(f32[64,256]{1,0:T(8,128)} %param.5) | copy-start | bytes 196612
  77.2 214.9 %all-gather.3.cloned.1.call-start = ((), (), s32[]{:S(2)}) async-start(), calls=%async_computation.4 | async-start | bytes 4325376 | tf_op jit(solution)/shard_map/all_gather | solution.py:69
  192.8 3.8 %copy-start.3 = (s32[64]{0:T(128)S(1)}, s32[64]{0:T(128)}, u32[]{:S(2)}) copy-start(s32[64]{0:T(128)} %param.7) | copy-start | bytes 772
  192.9 3.8 %copy-start.4 = (s32[64]{0:T(128)S(1)}, s32[64]{0:T(128)}, u32[]{:S(2)}) copy-start(s32[64]{0:T(128)} %param.6) | copy-start | bytes 772
  192.9 35.2 %all-to-all-start.1 = ((f32[256,8,256]{2,1,0:T(8,128)}), f32[256,8,256]{2,1,0:T(8,128)S(1)}, u32[]{:S(2)}, u32[]{:S(2)}) async-start(f32[256,8,256]{2,1,0:T(8,128)} %copy.21), calls=%async_computation.2 | async-start | bytes 4194304 | tf_op jit(solution)/shard_map/all_to_all | solution.py:65
  228.1 1.3 copy-start.1
  233.9 53.8 %collective-permute-start.1 = (f32[32,64,256]{2,1,0:T(8,128)}, f32[32,64,256]{2,1,0:T(8,128)}, u32[]{:S(2)}, u32[]{:S(2)}) collective-permute-start(f32[32,64,256]{2,1,0:T(8,128)} %pad_maximum_fusion.1), channel_id=1, source_target_pairs={{0,248},{8,0},{16,8},{24,16},{32,24},{40,32},{48,40},{56,48},{64,5... | collective-permute-start | bytes 6291464 | tf_op jit(solution)/shard_map/ppermute | solution.py:11
  241.2 46.5 %collective-permute-start = (f32[32,64,256]{2,1,0:T(8,128)}, f32[32,64,256]{2,1,0:T(8,128)}, u32[]{:S(2)}, u32[]{:S(2)}) collective-permute-start(f32[32,64,256]{2,1,0:T(8,128)} %pad_maximum_fusion), channel_id=1, source_target_pairs={{0,8},{8,16},{16,24},{24,32},{32,40},{40,48},{48,56},{56,64},{64,7... | collective-permute-start | bytes 6291464 | tf_op jit(solution)/shard_map/ppermute | solution.py:11
Sparse Core Ops, SparseCore 0:
  77.4 75.7 reduce-scatter.1
  155.0 68.0 all-gather.2
